TPU v7x, 512 devices: a whole 4x8x8 slice. The times are simulated.
512 devices in a mesh: seq: 64 (over y, x, core), head: 8 (over z).
Axes of the slice: x: 4, y: 8, z: 8, core: 2. Of those that a mesh axis runs over, the one named last changes fastest.
Arguments:
- queries: bfloat16 [2, 16384, 4096], P(None, ('seq', 'head')), may hold values from -6 to 6
- keys: bfloat16 [2, 16384, 4096], P(None, ('seq', 'head')), may hold values from -6 to 6
- values: bfloat16 [2, 16384, 4096], P(None, ('seq', 'head')), may hold values from -6 to 6
- rates: bfloat16 [2, 16384, 8], P(None, ('seq', 'head')), may hold values from 0.049804688 to 1
- fast_init: float32 [8, 3, 512, 256], P('head', None, 'seq'), may hold values from -0.25 to 0.25
Outputs:
- outputs: bfloat16 [2, 16384, 4096], P(None, 'seq', 'head')
All inputs are finite; a program needn't handle non-finite values.
Results may differ from a plain program's by a relative error of at most 0.0085.
Values may be sent and summed in bfloat16 or wider, within the bound.
A program may use at most 64 MiB of HBM per device.

v0:
```python
import jax
import jax.numpy as jnp
from jax import lax
from jax.experimental import pallas as pl
from jax.experimental.pallas import tpu as pltpu
from jax.sharding import Mesh
from jax.sharding import PartitionSpec as P

EPSILON = 1e-06
COEF_A = 3.4445
COEF_B = -4.775
COEF_C = 2.0315
LEARNING_STEP = 0.5
MESH = pl.DeviceIdType.MESH
BF16 = jnp.bfloat16
F32 = jnp.float32


def far_first(length):
    return sorted(range(1, length), key=lambda o: -min(o, length - o))


def dot_nt(a, b):
    return lax.dot_general(a, b, (((1,), (1,)), ((), ())), preferred_element_type=F32)


def dot_nn(a, b):
    return lax.dot_general(a, b, (((1,), (0,)), ((), ())), preferred_element_type=F32)


def remote(src, dst, send, recv, device):
    return pltpu.make_async_remote_copy(
        src_ref=src, dst_ref=dst, send_sem=send, recv_sem=recv,
        device_id=device, device_id_type=MESH,
    )


def make_kernel(sizes, blocks, tokens, hd, fh):
    ny, nx, nz = sizes
    half = fh // 2
    rows = 3 * half // ny
    cols = hd // nx
    wrows = hd // (nx * ny * 2)
    pieces = nx * ny

    def kernel(
        q_hbm, k_hbm, v_hbm, r_hbm, f_hbm, out_hbm,
        kbuf, dbuf, qbuf, vbuf, rbuf, dsrc, fpc, wag, gag, gsend, rx, ysend, ry,
        wf, wb, pbuf, obuf,
        zrecv, zsend, frecv, fsend, lsem, fpsem, xrecv, xsend, yrecv, ysem, arecv, asend,
    ):
        y, x, c, z = (lax.axis_index(a) for a in ("y", "x", "c", "z"))
        oc = 1 - c

        def at_y(o):
            return lax.rem(y + o, ny)

        def at_x(o):
            return lax.rem(x + o, nx)

        def at_z(o):
            return lax.rem(z + o, nz)

        barrier = pltpu.get_barrier_semaphore()
        greet = [{"z": at_z(o)} for o in range(1, nz)]
        greet += [{"x": at_x(o)} for o in range(1, nx)]
        greet += [{"y": at_y(o)} for o in range(1, ny)]
        greet += [{"c": oc}]

        load_v = pltpu.make_async_copy(v_hbm, vbuf, lsem.at[0])
        load_r = pltpu.make_async_copy(r_hbm, rbuf, lsem.at[1])
        load_f = pltpu.make_async_copy(
            f_hbm.at[0, :, :, pl.ds(pl.multiple_of(c * half, half), half)], fpc.at[c], lsem.at[2]
        )
        load_v.start()
        load_r.start()
        load_f.start()
        for device in greet:
            pl.semaphore_signal(barrier, inc=1, device_id=device, device_id_type=MESH)
        pl.semaphore_wait(barrier, len(greet))

        def head_columns(ref, b, t):
            return ref.at[b, :, pl.ds(pl.multiple_of(t * hd, hd), hd)]

        def z_send(kind, b, source, target):
            for o in far_first(nz):
                t = at_z(o)
                remote(source(t), target, zsend.at[kind, b], zrecv.at[kind, b, z], {"z": t}).start()
            pltpu.make_async_copy(source(z), target, zrecv.at[kind, b, z]).start()

        def z_wait(kind, b, target, zs):
            pltpu.make_async_copy(target, target, zrecv.at[kind, b, zs]).wait()

        def send_keys(b):
            z_send(0, b, lambda t: head_columns(k_hbm, b, t), kbuf.at[b, c, z])

        def send_grads(b):
            z_send(1, b, lambda t: dsrc.at[b, t], dbuf.at[b, c, z])

        def send_queries(b):
            z_send(2, b, lambda t: head_columns(q_hbm, b, t), qbuf.at[b, z])

        def scale_values(b):
            for h in range(nz):
                dsrc[b, h] = (
                    -(rbuf[b, :, h : h + 1].astype(F32) * vbuf[b, :, h * hd : (h + 1) * hd].astype(F32))
                ).astype(BF16)

        send_keys(0)
        f_copy = remote(
            f_hbm.at[0, :, :, pl.ds(pl.multiple_of(oc * half, half), half)],
            fpc.at[c], fpsem.at[0], fpsem.at[1], {"c": oc},
        )
        f_copy.start()
        load_v.wait()
        load_r.wait()
        scale_values(0)
        send_grads(0)

        def slot(cc, xx, yy):
            return (cc * nx + xx) * ny + yy

        def all_gather(which, buf):
            own = slot(c, x, y)
            send = asend.at[which]

            def give(s, device):
                remote(buf.at[s], buf.at[s], send, arecv.at[which, s], device).start()

            def take(s):
                remote(buf.at[s], buf.at[s], send, arecv.at[which, s], {"c": oc}).wait_recv()

            for o in far_first(ny):
                give(own, {"y": at_y(o)})
            for o in far_first(nx):
                give(own, {"x": at_x(o)})
            give(own, {"c": oc})
            for o in reversed(far_first(ny)):
                s = slot(c, x, at_y(o))
                take(s)
                for ox in far_first(nx):
                    give(s, {"x": at_x(ox)})
                give(s, {"c": oc})
            for o in [0] + list(reversed(far_first(ny))):
                for ox in reversed(far_first(nx)):
                    s = slot(c, at_x(ox), at_y(o))
                    take(s)
                    give(s, {"c": oc})
            for o in [0] + list(reversed(far_first(ny))):
                for ox in [0] + list(reversed(far_first(nx))):
                    take(slot(oc, at_x(ox), at_y(o)))

        load_f.wait()
        f_copy.wait_recv()
        wag[slot(c, x, y)] = jnp.concatenate([fpc[0], fpc[1]], axis=1).astype(BF16)
        all_gather(0, wag)
        for m in range(3):
            for cc in range(2):
                part = jnp.concatenate(
                    [wag[slot(cc, xx, yy), m] for yy in range(ny) for xx in range(nx)], axis=0
                )
                turned = part.T
                wb[m, cc] = turned
                wf[m, cc] = turned.astype(F32)

        for b in range(1, blocks):
            scale_values(b)

        def forward(b):
            for o in far_first(nz) + [0]:
                zs = lax.rem(z - o + nz, nz)
                for kind, buf in ((0, kbuf), (1, dbuf)):
                    mine = buf.at[b, c, zs]
                    z_wait(kind, b, mine, zs)
                    remote(
                        mine, mine, fsend.at[b, kind], frecv.at[b, kind, zs], {"c": oc}
                    ).start()

        def forwarded(b):
            for zs in range(nz):
                for kind, buf in ((0, kbuf), (1, dbuf)):
                    other = buf.at[b, oc, zs]
                    remote(other, other, fsend.at[b, kind], frecv.at[b, kind, zs], {"c": oc}).wait_recv()

        count = nz * tokens

        def hidden_parts(b, cc):
            keys = kbuf[b, cc].reshape(count, hd)
            out_grad = dbuf[b, cc].reshape(count, hd)
            gate_up = dot_nt(keys, jnp.concatenate([wb[0, c], wb[1, c]], axis=0))
            gate, up = gate_up[:, :half], gate_up[:, half:]
            hidden_grad = dot_nt(out_grad, wb[2, c])
            sig = jax.nn.sigmoid(gate)
            act = gate * sig
            slope = sig * (1.0 + gate * (1.0 - sig))
            at = pl.ds(pl.multiple_of(cc * count, count), count)
            pbuf[at, 0:half] = (hidden_grad * up * slope).astype(BF16)
            pbuf[at, half : 2 * half] = (hidden_grad * act).astype(BF16)
            pbuf[at, 2 * half : 3 * half] = (act * up).astype(BF16)

        def gradients(b):
            keys = kbuf[b].reshape(2 * count, hd)
            out_grad = dbuf[b].reshape(2 * count, hd)
            turned = pbuf[...].T
            both = jnp.concatenate(
                [dot_nn(turned[: 2 * half], keys), dot_nn(turned[2 * half :], out_grad)], axis=0
            )
            for xx in range(nx):
                gsend[b, xx] = both[:, xx * cols : (xx + 1) * cols].astype(BF16).reshape(ny, rows, cols)

        def start_reduce(b):
            for o in far_first(ny) + [0]:
                yr = at_y(o)
                for ox in far_first(nx):
                    xt = at_x(ox)
                    remote(
                        gsend.at[b, xt, yr], rx.at[b, ox - 1, yr],
                        xsend.at[b], xrecv.at[b, ox - 1, yr], {"x": xt},
                    ).start()

        def finish_reduce(b):
            total = None
            for o in far_first(ny) + [0]:
                yr = at_y(o)
                total = gsend[b, x, yr].astype(F32)
                for ox in range(1, nx):
                    land = rx.at[b, ox - 1, yr]
                    remote(land, land, xsend.at[b], xrecv.at[b, ox - 1, yr], {"c": oc}).wait_recv()
                    total = total + rx[b, ox - 1, yr].astype(F32)
                if o:
                    ysend[b, o - 1] = total.astype(BF16)
                    remote(
                        ysend.at[b, o - 1], ry.at[b, o - 1],
                        ysem.at[b], yrecv.at[b, o - 1], {"y": yr},
                    ).start()
            for o in far_first(ny):
                land = ry.at[b, o - 1]
                remote(land, land, ysem.at[b], yrecv.at[b, o - 1], {"c": oc}).wait_recv()
                total = total + ry[b, o - 1].astype(F32)
            gag[b, slot(c, x, y)] = total.astype(BF16)
            all_gather(1 + b, gag.at[b])

        def update(b):
            for m in range(3):
                low = jnp.concatenate(
                    [
                        jnp.concatenate(
                            [
                                gag[b, slot(cc, xx, 0) : slot(cc, xx, 0) + ny].reshape(3 * half, cols)[
                                    m * half : (m + 1) * half
                                ]
                                for xx in range(nx)
                            ],
                            axis=1,
                        )
                        for cc in range(2)
                    ],
                    axis=0,
                )
                full = low.astype(F32)
                inverse = 1.0 / (jnp.sqrt(jnp.sum(full * full, keepdims=True)) + EPSILON)
                gram = dot_nt(low, low) * (inverse * inverse)
                gram_low = gram.astype(BF16)
                poly = COEF_B * gram + COEF_C * dot_nn(gram_low, gram_low)
                first = (COEF_A * full + dot_nn(poly.astype(BF16), low)) * inverse
                first_low = first.astype(BF16)
                gram = dot_nt(first_low, first_low)
                gram_low = gram.astype(BF16)
                poly = COEF_B * gram + COEF_C * dot_nn(gram_low, gram_low)
                second = COEF_A * first + dot_nn(poly.astype(BF16), first_low)
                fresh = wf[m].reshape(fh, hd) - LEARNING_STEP * second
                wf[m] = fresh.reshape(2, half, hd)
                wb[m] = fresh.astype(BF16).reshape(2, half, hd)

        def out_copy(b):
            return pltpu.make_async_copy(obuf.at[b], out_hbm.at[b], lsem.at[3 + b])

        def answer(b):
            queries = qbuf[b].reshape(count, hd)
            gate = dot_nt(queries, wb[0].reshape(fh, hd))
            up = dot_nt(queries, wb[1].reshape(fh, hd))
            hidden = (gate * jax.nn.sigmoid(gate) * up).astype(BF16)
            obuf[b] = dot_nn(hidden, wb[2].reshape(fh, hd)).astype(BF16)
            out_copy(b).start()

        forward(0)
        for b in range(1, blocks):
            send_keys(b)
            send_grads(b)
        for b in range(blocks):
            send_queries(b)

        for b in range(blocks):
            hidden_parts(b, c)
            forwarded(b)
            hidden_parts(b, oc)
            gradients(b)
            start_reduce(b)
            if b:
                for zs in range(nz):
                    z_wait(2, b - 1, qbuf.at[b - 1, zs], zs)
                answer(b - 1)
            finish_reduce(b)
            if b + 1 < blocks:
                forward(b + 1)
            update(b)
        last = blocks - 1
        for zs in range(nz):
            z_wait(2, last, qbuf.at[last, zs], zs)
        answer(last)

        def sent(ref, sem):
            pltpu.make_async_copy(ref, ref, sem).wait()

        for b in range(blocks):
            for kind in range(3):
                sent(qbuf.at[0, 0 : nz - 1], zsend.at[kind, b])
            for kind in range(2):
                sent(kbuf.at[b, 0], fsend.at[b, kind])
            sent(gsend.at[b, 0 : nx - 1], xsend.at[b])
            sent(ysend.at[b], ysem.at[b])
            sent(gag.at[b, 0 : 2 * pieces - 1], asend.at[1 + b])
        sent(wag.at[0 : 2 * pieces - 1], asend.at[0])
        f_copy.wait_send()
        for b in range(blocks):
            out_copy(b).wait()

    dma = pltpu.SemaphoreType.DMA
    scratch = [
        pltpu.VMEM((blocks, 2, nz, tokens, hd), BF16),
        pltpu.VMEM((blocks, 2, nz, tokens, hd), BF16),
        pltpu.VMEM((blocks, nz, tokens, hd), BF16),
        pltpu.VMEM((blocks, tokens, nz * hd), BF16),
        pltpu.VMEM((blocks, tokens, nz), BF16),
        pltpu.VMEM((blocks, nz, tokens, hd), BF16),
        pltpu.VMEM((2, 3, wrows, half), F32),
        pltpu.VMEM((2 * pieces, 3, 2 * wrows, half), BF16),
        pltpu.VMEM((blocks, 2 * pieces, rows, cols), BF16),
        pltpu.VMEM((blocks, nx, ny, rows, cols), BF16),
        pltpu.VMEM((blocks, nx - 1, ny, rows, cols), BF16),
        pltpu.VMEM((blocks, ny - 1, rows, cols), BF16),
        pltpu.VMEM((blocks, ny - 1, rows, cols), BF16),
        pltpu.VMEM((3, 2, half, hd), F32),
        pltpu.VMEM((3, 2, half, hd), BF16),
        pltpu.VMEM((2 * nz * tokens, 3 * half), BF16),
        pltpu.VMEM((blocks, nz * tokens, hd), BF16),
        dma((3, blocks, nz)),
        dma((3, blocks)),
        dma((blocks, 2, nz)),
        dma((blocks, 2)),
        dma((3 + blocks,)),
        dma((2,)),
        dma((blocks, nx - 1, ny)),
        dma((blocks,)),
        dma((blocks, ny - 1)),
        dma((blocks,)),
        dma((1 + blocks, 2 * pieces)),
        dma((1 + blocks,)),
    ]
    return kernel, scratch


def build(mesh):
    ny, nx, _, nz = (mesh.shape[a] for a in ("y", "x", "c", "z"))

    def local(queries, keys, values, rates, fast_init):
        blocks, tokens, width = queries.shape
        hd = width // nz
        fh = fast_init.shape[3]
        kernel, scratch = make_kernel((ny, nx, nz), blocks, tokens, hd, fh)
        return pl.pallas_call(
            kernel,
            out_shape=jax.ShapeDtypeStruct((blocks, nz * tokens, hd), BF16),
            in_specs=[pl.BlockSpec(memory_space=pl.ANY)] * 5,
            out_specs=pl.BlockSpec(memory_space=pl.ANY),
            scratch_shapes=scratch,
            compiler_params=pltpu.CompilerParams(
                collective_id=0, has_side_effects=True, vmem_limit_bytes=60 * 1024 * 1024
            ),
        )(queries, keys, values, rates, fast_init)

    tokens_at = ("y", "x", "c", "z")
    in_specs = (
        P(None, tokens_at, None),
        P(None, tokens_at, None),
        P(None, tokens_at, None),
        P(None, tokens_at, None),
        P("z", None, ("y", "x", "c"), None),
    )
    out_specs = P(None, ("y", "x", "c"), "z")
    return jax.shard_map(local, mesh=mesh, in_specs=in_specs, out_specs=out_specs, check_vma=False)


def solution(mesh):
    seq, heads = mesh.shape["seq"], mesh.shape["head"]
    return build(Mesh(mesh.devices.reshape(seq // 8, 4, 2, heads), ("y", "x", "c", "z")))
```

profile of v0, /device:TPU:1, one launch (start us, length us, event | category | flops | bytes accessed | tf_op | source)
XLA Modules:
  0.0 87.4 jit_solution(5579274882676293940)
XLA Ops:
  0.0 1.4 %copy.6.r_hbm = bf16[2,32,8]{2,1,0:T(8,128)(2,1)} copy(bf16[2,32,8]{1,2,0:T(8,128)(2,1)} %param.8) | data formatting | bytes 2048 | tf_op args[3]
  1.4 84.1 %shard_map.55 = bf16[2,256,512]{2,1,0:T(8,128)(2,1)} custom-call(bf16[2,32,4096]{2,1,0:T(8,128)(2,1)} %q_hbm.1, bf16[2,32,4096]{2,1,0:T(8,128)(2,1)} %k_hbm.1, bf16[2,32,4096]{2,1,0:T(8,128)(2,1)} %v_hbm.1, bf16[2,32,8]{2,1,0:T(8,128)(2,1)} %copy.6.r_hbm, f32[1,3,8,256]{3,2,1,0:T(8,128)} %f_hbm.1), custom_call_target="tpu_custom_call" | custom-call | tf_op jit(solution)/shard_map/pallas_call | solution.py:371
  85.5 1.9 %copy.8 = bf16[2,256,512]{2,1,0:T(8,128)(2,1)} copy(bf16[2,256,512]{2,1,0:T(8,128)(2,1)} %shard_map.55) | data formatting | bytes 1048576
where the time goes:
time: 87.5 us; the launch traced here: 87.4 us
  Pallas kernels  84.1 us (96%)
  local copies, waits for them, and re-layouts  3.24 us (4%)
    pallas_call x1, Pallas kernels, local(): pl.pallas_call(kernel, out_shape=jax.ShapeDtypeStruct((blocks, nz * token...  84.1 us
    unnamed x2, local copies, waits for them, and re-layouts  3.24 us

commit v1 on v0

--- a/solution.py
+++ b/solution.py
@@ -44,9 +44,9 @@
     pieces = nx * ny
 
     def kernel(
-        q_hbm, k_hbm, v_hbm, r_hbm, f_hbm, out_hbm,
+        q_hbm, k_hbm, v_hbm, r_hbm, f_hbm, out_ref,
         kbuf, dbuf, qbuf, vbuf, rbuf, dsrc, fpc, wag, gag, gsend, rx, ysend, ry,
-        wf, wb, pbuf, obuf,
+        wf, wb, pbuf,
         zrecv, zsend, frecv, fsend, lsem, fpsem, xrecv, xsend, yrecv, ysem, arecv, asend,
     ):
         y, x, c, z = (lax.axis_index(a) for a in ("y", "x", "c", "z"))
@@ -101,9 +101,10 @@
             z_send(2, b, lambda t: head_columns(q_hbm, b, t), qbuf.at[b, z])
 
         def scale_values(b):
+            rate = rbuf[b].astype(F32).T
             for h in range(nz):
                 dsrc[b, h] = (
-                    -(rbuf[b, :, h : h + 1].astype(F32) * vbuf[b, :, h * hd : (h + 1) * hd].astype(F32))
+                    -(rate[:, h : h + 1] * vbuf[b, :, h * hd : (h + 1) * hd].astype(F32))
                 ).astype(BF16)
 
         send_keys(0)
@@ -241,47 +242,43 @@
             all_gather(1 + b, gag.at[b])
 
         def update(b):
+            lows = []
             for m in range(3):
-                low = jnp.concatenate(
-                    [
-                        jnp.concatenate(
-                            [
-                                gag[b, slot(cc, xx, 0) : slot(cc, xx, 0) + ny].reshape(3 * half, cols)[
-                                    m * half : (m + 1) * half
-                                ]
-                                for xx in range(nx)
-                            ],
-                            axis=1,
-                        )
-                        for cc in range(2)
-                    ],
-                    axis=0,
-                )
+                halves = []
+                for cc in range(2):
+                    parts = []
+                    for xx in range(nx):
+                        first_slot = slot(cc, xx, 0)
+                        whole = gag[b, first_slot : first_slot + ny].reshape(3 * half, cols)
+                        parts.append(whole[m * half : (m + 1) * half])
+                    halves.append(jnp.concatenate(parts, axis=1))
+                lows.append(jnp.concatenate(halves, axis=0))
+            grams = [dot_nt(low, low) for low in lows]
+            inverses = []
+            for low in lows:
                 full = low.astype(F32)
-                inverse = 1.0 / (jnp.sqrt(jnp.sum(full * full, keepdims=True)) + EPSILON)
-                gram = dot_nt(low, low) * (inverse * inverse)
-                gram_low = gram.astype(BF16)
-                poly = COEF_B * gram + COEF_C * dot_nn(gram_low, gram_low)
-                first = (COEF_A * full + dot_nn(poly.astype(BF16), low)) * inverse
-                first_low = first.astype(BF16)
-                gram = dot_nt(first_low, first_low)
-                gram_low = gram.astype(BF16)
-                poly = COEF_B * gram + COEF_C * dot_nn(gram_low, gram_low)
-                second = COEF_A * first + dot_nn(poly.astype(BF16), first_low)
+                inverses.append(1.0 / (jnp.sqrt(jnp.sum(full * full, keepdims=True)) + EPSILON))
+            grams = [g * (i * i) for g, i in zip(grams, inverses)]
+            polys = [COEF_B * g + COEF_C * dot_nn(g.astype(BF16), g.astype(BF16)) for g in grams]
+            firsts = [
+                (COEF_A * low.astype(F32) + dot_nn(p.astype(BF16), low)) * i
+                for low, p, i in zip(lows, polys, inverses)
+            ]
+            first_lows = [f.astype(BF16) for f in firsts]
+            grams = [dot_nt(f, f) for f in first_lows]
+            polys = [COEF_B * g + COEF_C * dot_nn(g.astype(BF16), g.astype(BF16)) for g in grams]
+            for m in range(3):
+                second = COEF_A * firsts[m] + dot_nn(polys[m].astype(BF16), first_lows[m])
                 fresh = wf[m].reshape(fh, hd) - LEARNING_STEP * second
                 wf[m] = fresh.reshape(2, half, hd)
                 wb[m] = fresh.astype(BF16).reshape(2, half, hd)
-
-        def out_copy(b):
-            return pltpu.make_async_copy(obuf.at[b], out_hbm.at[b], lsem.at[3 + b])
 
         def answer(b):
             queries = qbuf[b].reshape(count, hd)
             gate = dot_nt(queries, wb[0].reshape(fh, hd))
             up = dot_nt(queries, wb[1].reshape(fh, hd))
             hidden = (gate * jax.nn.sigmoid(gate) * up).astype(BF16)
-            obuf[b] = dot_nn(hidden, wb[2].reshape(fh, hd)).astype(BF16)
-            out_copy(b).start()
+            out_ref[b] = dot_nn(hidden, wb[2].reshape(fh, hd)).astype(BF16)
 
         forward(0)
         for b in range(1, blocks):
@@ -322,8 +319,6 @@
             sent(gag.at[b, 0 : 2 * pieces - 1], asend.at[1 + b])
         sent(wag.at[0 : 2 * pieces - 1], asend.at[0])
         f_copy.wait_send()
-        for b in range(blocks):
-            out_copy(b).wait()
 
     dma = pltpu.SemaphoreType.DMA
     scratch = [
@@ -331,7 +326,7 @@
         pltpu.VMEM((blocks, 2, nz, tokens, hd), BF16),
         pltpu.VMEM((blocks, nz, tokens, hd), BF16),
         pltpu.VMEM((blocks, tokens, nz * hd), BF16),
-        pltpu.VMEM((blocks, tokens, nz), BF16),
+        pltpu.VMEM((blocks, nz, tokens), BF16),
         pltpu.VMEM((blocks, nz, tokens, hd), BF16),
         pltpu.VMEM((2, 3, wrows, half), F32),
         pltpu.VMEM((2 * pieces, 3, 2 * wrows, half), BF16),
@@ -343,12 +338,11 @@
         pltpu.VMEM((3, 2, half, hd), F32),
         pltpu.VMEM((3, 2, half, hd), BF16),
         pltpu.VMEM((2 * nz * tokens, 3 * half), BF16),
-        pltpu.VMEM((blocks, nz * tokens, hd), BF16),
         dma((3, blocks, nz)),
         dma((3, blocks)),
         dma((blocks, 2, nz)),
         dma((blocks, 2)),
-        dma((3 + blocks,)),
+        dma((3,)),
         dma((2,)),
         dma((blocks, nx - 1, ny)),
         dma((blocks,)),
@@ -370,14 +364,14 @@
         kernel, scratch = make_kernel((ny, nx, nz), blocks, tokens, hd, fh)
         return pl.pallas_call(
             kernel,
-            out_shape=jax.ShapeDtypeStruct((blocks, nz * tokens, hd), BF16),
+            out_shape=pltpu.VMEM((blocks, nz * tokens, hd), BF16),
             in_specs=[pl.BlockSpec(memory_space=pl.ANY)] * 5,
-            out_specs=pl.BlockSpec(memory_space=pl.ANY),
+            out_specs=pl.BlockSpec(memory_space=pltpu.VMEM),
             scratch_shapes=scratch,
             compiler_params=pltpu.CompilerParams(
                 collective_id=0, has_side_effects=True, vmem_limit_bytes=60 * 1024 * 1024
             ),
-        )(queries, keys, values, rates, fast_init)
+        )(queries, keys, values, jnp.swapaxes(rates, 1, 2), fast_init)
 
     tokens_at = ("y", "x", "c", "z")
     in_specs = (

time: 87.5 us -> 80.2 us (0.917)
  Pallas kernels: 84.1 us -> 79.3 us
  local copies, waits for them, and re-layouts: 3.24 us -> 0.8 us
    pallas_call x1, Pallas kernels: 84.1 us -> 79.3 us  [local(): pl.pallas_call(kernel, out_shape=pltpu.VMEM((blocks, nz * tokens, hd), BF...]
    unnamed x2 -> x1, local copies, waits for them, and re-layouts: 3.24 us -> 0.8 us
where the time goes in v1:
time: 80.2 us; the launch traced here: 80.1 us
  Pallas kernels  79.3 us (99%)
    pallas_call x1, Pallas kernels, local(): pl.pallas_call(kernel, out_shape=pltpu.VMEM((blocks, nz * tokens, hd), BF...  79.3 us

profile of v1, /device:TPU:1, one launch (start us, length us, event | category | flops | bytes accessed | tf_op | source)
XLA Modules:
  0.0 80.1 jit_solution(6877145983399864961)
XLA Ops:
  0.0 79.3 %shard_map.55 = bf16[2,256,512]{2,1,0:T(8,128)(2,1)S(1)} custom-call(bf16[2,32,4096]{2,1,0:T(8,128)(2,1)} %q_hbm.1, bf16[2,32,4096]{2,1,0:T(8,128)(2,1)} %k_hbm.1, bf16[2,32,4096]{2,1,0:T(8,128)(2,1)} %v_hbm.1, bf16[2,8,32]{2,1,0:T(8,128)(2,1)} %bitcast.1, f32[1,3,8,256]{3,2,1,0:T(8,128)} %f_hbm.1), custom_call_target="tpu_custom_call" | custom-call | tf_op jit(solution)/shard_map/pallas_call | solution.py:365
  79.3 0.8 copy.7

commit v2 on v1

--- a/solution.py
+++ b/solution.py
@@ -38,16 +38,21 @@
 def make_kernel(sizes, blocks, tokens, hd, fh):
     ny, nx, nz = sizes
     half = fh // 2
-    rows = 3 * half // ny
+    rows = 2 * half // ny
+    rest = half // ny
     cols = hd // nx
     wrows = hd // (nx * ny * 2)
     pieces = nx * ny
 
     def kernel(
         q_hbm, k_hbm, v_hbm, r_hbm, f_hbm, out_ref,
-        kbuf, dbuf, qbuf, vbuf, rbuf, dsrc, fpc, wag, gag, gsend, rx, ysend, ry,
-        wf, wb, pbuf,
-        zrecv, zsend, frecv, fsend, lsem, fpsem, xrecv, xsend, yrecv, ysem, arecv, asend,
+        kbuf, dbuf, qbuf, vbuf, rbuf, dsrc, fpc, wag,
+        a_send, a_land, a_send2, a_land2, a_all,
+        b_send, b_land, b_send2, b_land2, b_all,
+        wf, wb, pbuf, acts, slopes,
+        zrecv, zsend, frecv, fsend, lsem, fpsem, wrecv, wsend,
+        a_recv1, a_sem1, a_recv2, a_sem2, a_recv3, a_sem3,
+        b_recv1, b_sem1, b_recv2, b_sem2, b_recv3, b_sem3,
     ):
         y, x, c, z = (lax.axis_index(a) for a in ("y", "x", "c", "z"))
         oc = 1 - c
@@ -113,48 +118,121 @@
             fpc.at[c], fpsem.at[0], fpsem.at[1], {"c": oc},
         )
         f_copy.start()
+
+        def slot(cc, xx, yy):
+            return (cc * nx + xx) * ny + yy
+
+        def across_y(o):
+            return {"y": at_y(o)}
+
+        def across_x(o):
+            return {"x": at_x(o)}
+
+        def slot_y(cc, oy, ox):
+            return slot(cc, at_x(ox), at_y(oy))
+
+        def slot_x(cc, ox, oy):
+            return slot(cc, at_x(ox), at_y(oy))
+
+        class Gather:
+            def __init__(self, buf, send, recv, n1, peer1, n2, peer2, place):
+                self.buf, self.send, self.recv, self.place = buf, send, recv, place
+                self.n1, self.peer1, self.n2, self.peer2 = n1, peer1, n2, peer2
+                self.own = place(c, 0, 0)
+
+            def give(self, s, device):
+                remote(self.buf.at[s], self.buf.at[s], self.send, self.recv.at[s], device).start()
+
+            def take(self, s):
+                remote(self.buf.at[s], self.buf.at[s], self.send, self.recv.at[s], {"c": oc}).wait_recv()
+
+            def start1(self):
+                for o in far_first(self.n1):
+                    self.give(self.own, self.peer1(o))
+
+            def start2(self):
+                for o in far_first(self.n2):
+                    self.give(self.own, self.peer2(o))
+                self.give(self.own, {"c": oc})
+
+            def relay1(self):
+                for o in reversed(far_first(self.n1)):
+                    s = self.place(c, o, 0)
+                    self.take(s)
+                    for o2 in far_first(self.n2):
+                        self.give(s, self.peer2(o2))
+                    self.give(s, {"c": oc})
+                    yield
+
+            def relay2(self):
+                for o in [0] + list(reversed(far_first(self.n1))):
+                    for o2 in reversed(far_first(self.n2)):
+                        s = self.place(c, o, o2)
+                        self.take(s)
+                        self.give(s, {"c": oc})
+                        yield
+
+            def end(self):
+                for o in [0] + list(reversed(far_first(self.n1))):
+                    for o2 in [0] + list(reversed(far_first(self.n2))):
+                        self.take(self.place(oc, o, o2))
+
+        def run(*pairs):
+            live = list(pairs)
+            while live:
+                for pair in list(live):
+                    steps, many = pair
+                    for _ in range(many):
+                        try:
+                            next(steps)
+                        except StopIteration:
+                            live.remove(pair)
+                            break
+
+        load_f.wait()
+        f_copy.wait_recv()
+        wag[slot(c, x, y)] = jnp.concatenate([fpc[0], fpc[1]], axis=1).astype(BF16)
+        weights_gather = Gather(wag, wsend, wrecv, ny, across_y, nx, across_x, slot_y)
+        weights_gather.start1()
+        weights_gather.start2()
         load_v.wait()
         load_r.wait()
         scale_values(0)
         send_grads(0)
-
-        def slot(cc, xx, yy):
-            return (cc * nx + xx) * ny + yy
-
-        def all_gather(which, buf):
-            own = slot(c, x, y)
-            send = asend.at[which]
-
-            def give(s, device):
-                remote(buf.at[s], buf.at[s], send, arecv.at[which, s], device).start()
-
-            def take(s):
-                remote(buf.at[s], buf.at[s], send, arecv.at[which, s], {"c": oc}).wait_recv()
-
-            for o in far_first(ny):
-                give(own, {"y": at_y(o)})
-            for o in far_first(nx):
-                give(own, {"x": at_x(o)})
-            give(own, {"c": oc})
-            for o in reversed(far_first(ny)):
-                s = slot(c, x, at_y(o))
-                take(s)
-                for ox in far_first(nx):
-                    give(s, {"x": at_x(ox)})
-                give(s, {"c": oc})
-            for o in [0] + list(reversed(far_first(ny))):
-                for ox in reversed(far_first(nx)):
-                    s = slot(c, at_x(ox), at_y(o))
-                    take(s)
-                    give(s, {"c": oc})
-            for o in [0] + list(reversed(far_first(ny))):
-                for ox in [0] + list(reversed(far_first(nx))):
-                    take(slot(oc, at_x(ox), at_y(o)))
-
-        load_f.wait()
-        f_copy.wait_recv()
-        wag[slot(c, x, y)] = jnp.concatenate([fpc[0], fpc[1]], axis=1).astype(BF16)
-        all_gather(0, wag)
+        run((weights_gather.relay1(), 1))
+        run((weights_gather.relay2(), 1))
+
+        def forward(b, kind, buf):
+            for o in far_first(nz) + [0]:
+                zs = lax.rem(z - o + nz, nz)
+                mine = buf.at[b, c, zs]
+                z_wait(kind, b, mine, zs)
+                remote(mine, mine, fsend.at[b, kind], frecv.at[b, kind, zs], {"c": oc}).start()
+
+        def forwarded(b, kind, buf):
+            for zs in range(nz):
+                other = buf.at[b, oc, zs]
+                remote(other, other, fsend.at[b, kind], frecv.at[b, kind, zs], {"c": oc}).wait_recv()
+
+        count = nz * tokens
+
+        def keys_part(b, cc):
+            keys = kbuf[b, cc].reshape(count, hd)
+            gate_up = dot_nt(keys, jnp.concatenate([wb[0, c], wb[1, c]], axis=0))
+            gate, up = gate_up[:, :half], gate_up[:, half:]
+            sig = jax.nn.sigmoid(gate)
+            act = gate * sig
+            acts[cc] = act
+            slopes[cc] = up * (sig * (1.0 + gate * (1.0 - sig)))
+            pbuf[cc, :, 2 * half : 3 * half] = (act * up).astype(BF16)
+
+        def grads_part(b, cc):
+            hidden_grad = dot_nt(dbuf[b, cc].reshape(count, hd), wb[2, c])
+            pbuf[cc, :, 0:half] = (hidden_grad * slopes[cc]).astype(BF16)
+            pbuf[cc, :, half : 2 * half] = (hidden_grad * acts[cc]).astype(BF16)
+
+        forward(0, 0, kbuf)
+        weights_gather.end()
         for m in range(3):
             for cc in range(2):
                 part = jnp.concatenate(
@@ -163,83 +241,93 @@
                 turned = part.T
                 wb[m, cc] = turned
                 wf[m, cc] = turned.astype(F32)
-
-        for b in range(1, blocks):
-            scale_values(b)
-
-        def forward(b):
-            for o in far_first(nz) + [0]:
-                zs = lax.rem(z - o + nz, nz)
-                for kind, buf in ((0, kbuf), (1, dbuf)):
-                    mine = buf.at[b, c, zs]
-                    z_wait(kind, b, mine, zs)
-                    remote(
-                        mine, mine, fsend.at[b, kind], frecv.at[b, kind, zs], {"c": oc}
-                    ).start()
-
-        def forwarded(b):
-            for zs in range(nz):
-                for kind, buf in ((0, kbuf), (1, dbuf)):
-                    other = buf.at[b, oc, zs]
-                    remote(other, other, fsend.at[b, kind], frecv.at[b, kind, zs], {"c": oc}).wait_recv()
-
-        count = nz * tokens
-
-        def hidden_parts(b, cc):
-            keys = kbuf[b, cc].reshape(count, hd)
-            out_grad = dbuf[b, cc].reshape(count, hd)
-            gate_up = dot_nt(keys, jnp.concatenate([wb[0, c], wb[1, c]], axis=0))
-            gate, up = gate_up[:, :half], gate_up[:, half:]
-            hidden_grad = dot_nt(out_grad, wb[2, c])
-            sig = jax.nn.sigmoid(gate)
-            act = gate * sig
-            slope = sig * (1.0 + gate * (1.0 - sig))
-            at = pl.ds(pl.multiple_of(cc * count, count), count)
-            pbuf[at, 0:half] = (hidden_grad * up * slope).astype(BF16)
-            pbuf[at, half : 2 * half] = (hidden_grad * act).astype(BF16)
-            pbuf[at, 2 * half : 3 * half] = (act * up).astype(BF16)
+        keys_part(0, c)
+        forwarded(0, 0, kbuf)
+        keys_part(0, oc)
+        forward(0, 1, dbuf)
 
         def gradients(b):
             keys = kbuf[b].reshape(2 * count, hd)
             out_grad = dbuf[b].reshape(2 * count, hd)
-            turned = pbuf[...].T
-            both = jnp.concatenate(
-                [dot_nn(turned[: 2 * half], keys), dot_nn(turned[2 * half :], out_grad)], axis=0
+            turned = pbuf[...].reshape(2 * count, 3 * half).T
+            third = dot_nn(turned[2 * half :], out_grad)
+            for xx in range(nx):
+                b_send[b, :, xx] = third[:, xx * cols : (xx + 1) * cols].astype(BF16).reshape(ny, rest, cols)
+            both = dot_nn(turned[: 2 * half], keys)
+            for xx in range(nx):
+                a_send[b, xx] = both[:, xx * cols : (xx + 1) * cols].astype(BF16).reshape(ny, rows, cols)
+
+        class Reduce:
+            def __init__(self, b, bufs, sems, n1, at1, name1, me1, n2, at2, name2):
+                self.send, self.land, self.send2, self.land2 = (r.at[b] for r in bufs)
+                self.recv1, self.sem1, self.recv2, self.sem2 = (r.at[b] for r in sems)
+                self.n1, self.at1, self.name1, self.me1 = n1, at1, name1, me1
+                self.n2, self.at2, self.name2 = n2, at2, name2
+
+            def start(self):
+                for o in far_first(self.n2) + [0]:
+                    end = self.at2(o)
+                    for o1 in far_first(self.n1):
+                        t = self.at1(o1)
+                        remote(
+                            self.send.at[t, end], self.land.at[o1 - 1, end],
+                            self.sem1, self.recv1.at[o1 - 1, end], {self.name1: t},
+                        ).start()
+
+            def steps(self, result, where):
+                total = None
+                for o in far_first(self.n2) + [0]:
+                    end = self.at2(o)
+                    total = self.send[self.me1, end].astype(F32)
+                    for o1 in range(1, self.n1):
+                        land = self.land.at[o1 - 1, end]
+                        remote(land, land, self.sem1, self.recv1.at[o1 - 1, end], {"c": oc}).wait_recv()
+                        total = total + land[...].astype(F32)
+                    if o:
+                        self.send2[o - 1] = total.astype(BF16)
+                        remote(
+                            self.send2.at[o - 1], self.land2.at[o - 1],
+                            self.sem2, self.recv2.at[o - 1], {self.name2: end},
+                        ).start()
+                    yield
+                for o in far_first(self.n2):
+                    land = self.land2.at[o - 1]
+                    remote(land, land, self.sem2, self.recv2.at[o - 1], {"c": oc}).wait_recv()
+                    total = total + land[...].astype(F32)
+                    yield
+                result[where] = total.astype(BF16)
+
+        def sums(b):
+            return (
+                Reduce(
+                    b, (a_send, a_land, a_send2, a_land2), (a_recv1, a_sem1, a_recv2, a_sem2),
+                    nx, at_x, "x", x, ny, at_y, "y",
+                ),
+                Reduce(
+                    b, (b_send, b_land, b_send2, b_land2), (b_recv1, b_sem1, b_recv2, b_sem2),
+                    ny, at_y, "y", y, nx, at_x, "x",
+                ),
             )
-            for xx in range(nx):
-                gsend[b, xx] = both[:, xx * cols : (xx + 1) * cols].astype(BF16).reshape(ny, rows, cols)
 
         def start_reduce(b):
-            for o in far_first(ny) + [0]:
-                yr = at_y(o)
-                for ox in far_first(nx):
-                    xt = at_x(ox)
-                    remote(
-                        gsend.at[b, xt, yr], rx.at[b, ox - 1, yr],
-                        xsend.at[b], xrecv.at[b, ox - 1, yr], {"x": xt},
-                    ).start()
+            for part in reversed(sums(b)):
+                part.start()
 
         def finish_reduce(b):
-            total = None
-            for o in far_first(ny) + [0]:
-                yr = at_y(o)
-                total = gsend[b, x, yr].astype(F32)
-                for ox in range(1, nx):
-                    land = rx.at[b, ox - 1, yr]
-                    remote(land, land, xsend.at[b], xrecv.at[b, ox - 1, yr], {"c": oc}).wait_recv()
-                    total = total + rx[b, ox - 1, yr].astype(F32)
-                if o:
-                    ysend[b, o - 1] = total.astype(BF16)
-                    remote(
-                        ysend.at[b, o - 1], ry.at[b, o - 1],
-                        ysem.at[b], yrecv.at[b, o - 1], {"y": yr},
-                    ).start()
-            for o in far_first(ny):
-                land = ry.at[b, o - 1]
-                remote(land, land, ysem.at[b], yrecv.at[b, o - 1], {"c": oc}).wait_recv()
-                total = total + ry[b, o - 1].astype(F32)
-            gag[b, slot(c, x, y)] = total.astype(BF16)
-            all_gather(1 + b, gag.at[b])
+            first, second = sums(b)
+            own = slot(c, x, y)
+            run((first.steps(a_all.at[b], own), 2), (second.steps(b_all.at[b], own), 1))
+            ga = Gather(a_all.at[b], a_sem3.at[b], a_recv3.at[b], ny, across_y, nx, across_x, slot_y)
+            gb = Gather(b_all.at[b], b_sem3.at[b], b_recv3.at[b], nx, across_x, ny, across_y, slot_x)
+            ga.start1()
+            gb.start1()
+            ga.start2()
+            gb.start2()
+            run((gb.relay1(), 1))
+            run((ga.relay1(), 1))
+            run((ga.relay2(), 1), (gb.relay2(), 1))
+            ga.end()
+            gb.end()
 
         def update(b):
             lows = []
@@ -249,8 +337,11 @@
                     parts = []
                     for xx in range(nx):
                         first_slot = slot(cc, xx, 0)
-                        whole = gag[b, first_slot : first_slot + ny].reshape(3 * half, cols)
-                        parts.append(whole[m * half : (m + 1) * half])
+                        if m < 2:
+                            whole = a_all[b, first_slot : first_slot + ny].reshape(2 * half, cols)
+                            parts.append(whole[m * half : (m + 1) * half])
+                        else:
+                            parts.append(b_all[b, first_slot : first_slot + ny].reshape(half, cols))
                     halves.append(jnp.concatenate(parts, axis=1))
                 lows.append(jnp.concatenate(halves, axis=0))
             grams = [dot_nt(low, low) for low in lows]
@@ -280,27 +371,34 @@
             hidden = (gate * jax.nn.sigmoid(gate) * up).astype(BF16)
             out_ref[b] = dot_nn(hidden, wb[2].reshape(fh, hd)).astype(BF16)
 
-        forward(0)
         for b in range(1, blocks):
             send_keys(b)
-            send_grads(b)
+
         for b in range(blocks):
-            send_queries(b)
-
-        for b in range(blocks):
-            hidden_parts(b, c)
-            forwarded(b)
-            hidden_parts(b, oc)
+            grads_part(b, c)
+            forwarded(b, 1, dbuf)
+            grads_part(b, oc)
             gradients(b)
             start_reduce(b)
-            if b:
+            if b == 0:
+                for later in range(1, blocks):
+                    scale_values(later)
+                    send_grads(later)
+                for each in range(blocks):
+                    send_queries(each)
+            else:
                 for zs in range(nz):
                     z_wait(2, b - 1, qbuf.at[b - 1, zs], zs)
                 answer(b - 1)
             finish_reduce(b)
             if b + 1 < blocks:
-                forward(b + 1)
+                forward(b + 1, 0, kbuf)
+                forward(b + 1, 1, dbuf)
             update(b)
+            if b + 1 < blocks:
+                keys_part(b + 1, c)
+                forwarded(b + 1, 0, kbuf)
+                keys_part(b + 1, oc)
         last = blocks - 1
         for zs in range(nz):
             z_wait(2, last, qbuf.at[last, zs], zs)
@@ -314,10 +412,13 @@
                 sent(qbuf.at[0, 0 : nz - 1], zsend.at[kind, b])
             for kind in range(2):
                 sent(kbuf.at[b, 0], fsend.at[b, kind])
-            sent(gsend.at[b, 0 : nx - 1], xsend.at[b])
-            sent(ysend.at[b], ysem.at[b])
-            sent(gag.at[b, 0 : 2 * pieces - 1], asend.at[1 + b])
-        sent(wag.at[0 : 2 * pieces - 1], asend.at[0])
+            sent(a_send.at[b, 0 : nx - 1], a_sem1.at[b])
+            sent(b_send.at[b, 0 : ny - 1], b_sem1.at[b])
+            sent(a_send2.at[b], a_sem2.at[b])
+            sent(b_send2.at[b], b_sem2.at[b])
+            sent(a_all.at[b, 0 : 2 * pieces - 1], a_sem3.at[b])
+            sent(b_all.at[b, 0 : 2 * pieces - 1], b_sem3.at[b])
+        sent(wag.at[0 : 2 * pieces - 1], wsend)
         f_copy.wait_send()
 
     dma = pltpu.SemaphoreType.DMA
@@ -330,26 +431,41 @@
         pltpu.VMEM((blocks, nz, tokens, hd), BF16),
         pltpu.VMEM((2, 3, wrows, half), F32),
         pltpu.VMEM((2 * pieces, 3, 2 * wrows, half), BF16),
-        pltpu.VMEM((blocks, 2 * pieces, rows, cols), BF16),
         pltpu.VMEM((blocks, nx, ny, rows, cols), BF16),
         pltpu.VMEM((blocks, nx - 1, ny, rows, cols), BF16),
         pltpu.VMEM((blocks, ny - 1, rows, cols), BF16),
         pltpu.VMEM((blocks, ny - 1, rows, cols), BF16),
+        pltpu.VMEM((blocks, 2 * pieces, rows, cols), BF16),
+        pltpu.VMEM((blocks, ny, nx, rest, cols), BF16),
+        pltpu.VMEM((blocks, ny - 1, nx, rest, cols), BF16),
+        pltpu.VMEM((blocks, nx - 1, rest, cols), BF16),
+        pltpu.VMEM((blocks, nx - 1, rest, cols), BF16),
+        pltpu.VMEM((blocks, 2 * pieces, rest, cols), BF16),
         pltpu.VMEM((3, 2, half, hd), F32),
         pltpu.VMEM((3, 2, half, hd), BF16),
-        pltpu.VMEM((2 * nz * tokens, 3 * half), BF16),
+        pltpu.VMEM((2, nz * tokens, 3 * half), BF16),
+        pltpu.VMEM((2, nz * tokens, half), F32),
+        pltpu.VMEM((2, nz * tokens, half), F32),
         dma((3, blocks, nz)),
         dma((3, blocks)),
         dma((blocks, 2, nz)),
         dma((blocks, 2)),
         dma((3,)),
         dma((2,)),
+        dma((2 * pieces,)),
+        dma(()),
         dma((blocks, nx - 1, ny)),
         dma((blocks,)),
         dma((blocks, ny - 1)),
         dma((blocks,)),
-        dma((1 + blocks, 2 * pieces)),
-        dma((1 + blocks,)),
+        dma((blocks, 2 * pieces)),
+        dma((blocks,)),
+        dma((blocks, ny - 1, nx)),
+        dma((blocks,)),
+        dma((blocks, nx - 1)),
+        dma((blocks,)),
+        dma((blocks, 2 * pieces)),
+        dma((blocks,)),
     ]
     return kernel, scratch
 

time: 80.2 us -> 78.9 us (0.984)
  Pallas kernels: 79.3 us -> 77.9 us
    pallas_call x1, Pallas kernels: 79.3 us -> 77.9 us  [local(): pl.pallas_call(kernel, out_shape=pltpu.VMEM((blocks, nz * tokens, hd), BF...]
where the time goes in v2:
time: 78.9 us; the launch traced here: 78.7 us
  Pallas kernels  77.9 us (99%)
  local copies, waits for them, and re-layouts  0.8 us (1%)
    pallas_call x1, Pallas kernels, local(): pl.pallas_call(kernel, out_shape=pltpu.VMEM((blocks, nz * tokens, hd), BF...  77.9 us

profile of v2, /device:TPU:1, one launch (start us, length us, event | category | flops | bytes accessed | tf_op | source)
XLA Modules:
  0.0 78.7 jit_solution(14267929164254798139)
XLA Ops:
  0.0 77.9 %shard_map.55 = bf16[2,256,512]{2,1,0:T(8,128)(2,1)S(1)} custom-call(bf16[2,32,4096]{2,1,0:T(8,128)(2,1)} %q_hbm.1, bf16[2,32,4096]{2,1,0:T(8,128)(2,1)} %k_hbm.1, bf16[2,32,4096]{2,1,0:T(8,128)(2,1)} %v_hbm.1, bf16[2,8,32]{2,1,0:T(8,128)(2,1)} %bitcast.1, f32[1,3,8,256]{3,2,1,0:T(8,128)} %f_hbm.1), custom_call_target="tpu_custom_call" | custom-call | tf_op jit(solution)/shard_map/pallas_call | solution.py:481
  78.0 0.8 %copy.7 = bf16[2,256,512]{2,1,0:T(8,128)(2,1)} copy(bf16[2,256,512]{2,1,0:T(8,128)(2,1)S(1)} %shard_map.55) | data formatting | bytes 1048576

commit v3 on v2

--- a/solution.py
+++ b/solution.py
@@ -50,7 +50,7 @@
         a_send, a_land, a_send2, a_land2, a_all,
         b_send, b_land, b_send2, b_land2, b_all,
         wf, wb, pbuf, acts, slopes,
-        zrecv, zsend, frecv, fsend, lsem, fpsem, wrecv, wsend,
+        zall, zfirst, zsend, frecv, fsend, lsem, fpsem, wrecv, wsend,
         a_recv1, a_sem1, a_recv2, a_sem2, a_recv3, a_sem3,
         b_recv1, b_sem1, b_recv2, b_sem2, b_recv3, b_sem3,
     ):
@@ -87,14 +87,17 @@
         def head_columns(ref, b, t):
             return ref.at[b, :, pl.ds(pl.multiple_of(t * hd, hd), hd)]
 
+        def z_sem(kind, b):
+            return zfirst.at[z] if (kind, b) == (1, 0) else zall.at[kind, b]
+
+        def arrived(ref, sem):
+            pltpu.make_async_copy(ref, ref, sem).wait()
+
         def z_send(kind, b, source, target):
             for o in far_first(nz):
                 t = at_z(o)
-                remote(source(t), target, zsend.at[kind, b], zrecv.at[kind, b, z], {"z": t}).start()
-            pltpu.make_async_copy(source(z), target, zrecv.at[kind, b, z]).start()
-
-        def z_wait(kind, b, target, zs):
-            pltpu.make_async_copy(target, target, zrecv.at[kind, b, zs]).wait()
+                remote(source(t), target, zsend.at[kind, b], z_sem(kind, b), {"z": t}).start()
+            pltpu.make_async_copy(source(z), target, z_sem(kind, b)).start()
 
         def send_keys(b):
             z_send(0, b, lambda t: head_columns(k_hbm, b, t), kbuf.at[b, c, z])
@@ -135,47 +138,42 @@
             return slot(cc, at_x(ox), at_y(oy))
 
         class Gather:
-            def __init__(self, buf, send, recv, n1, peer1, n2, peer2, place):
+            def __init__(self, buf, send, recv, n1, at1, peer1, n2, peer2, place):
                 self.buf, self.send, self.recv, self.place = buf, send, recv, place
-                self.n1, self.peer1, self.n2, self.peer2 = n1, peer1, n2, peer2
+                self.n1, self.at1, self.peer1, self.n2, self.peer2 = n1, at1, peer1, n2, peer2
                 self.own = place(c, 0, 0)
 
-            def give(self, s, device):
-                remote(self.buf.at[s], self.buf.at[s], self.send, self.recv.at[s], device).start()
-
-            def take(self, s):
-                remote(self.buf.at[s], self.buf.at[s], self.send, self.recv.at[s], {"c": oc}).wait_recv()
+            def give(self, s, device, sem):
+                remote(self.buf.at[s], self.buf.at[s], self.send, self.recv.at[sem], device).start()
 
             def start1(self):
                 for o in far_first(self.n1):
-                    self.give(self.own, self.peer1(o))
+                    self.give(self.own, self.peer1(o), self.at1(0))
+
+            def spread(self, s, o):
+                for o2 in far_first(self.n2):
+                    self.give(s, self.peer2(o2), self.n1 + self.at1(o))
+                self.give(s, {"c": oc}, 2 * self.n1)
 
             def start2(self):
-                for o in far_first(self.n2):
-                    self.give(self.own, self.peer2(o))
-                self.give(self.own, {"c": oc})
+                self.spread(self.own, 0)
 
             def relay1(self):
                 for o in reversed(far_first(self.n1)):
                     s = self.place(c, o, 0)
-                    self.take(s)
-                    for o2 in far_first(self.n2):
-                        self.give(s, self.peer2(o2))
-                    self.give(s, {"c": oc})
+                    arrived(self.buf.at[s], self.recv.at[self.at1(o)])
+                    self.spread(s, o)
                     yield
 
             def relay2(self):
                 for o in [0] + list(reversed(far_first(self.n1))):
-                    for o2 in reversed(far_first(self.n2)):
-                        s = self.place(c, o, o2)
-                        self.take(s)
-                        self.give(s, {"c": oc})
-                        yield
+                    arrived(self.buf.at[0 : self.n2 - 1], self.recv.at[self.n1 + self.at1(o)])
+                    for o2 in far_first(self.n2):
+                        self.give(self.place(c, o, o2), {"c": oc}, 2 * self.n1)
+                    yield
 
             def end(self):
-                for o in [0] + list(reversed(far_first(self.n1))):
-                    for o2 in [0] + list(reversed(far_first(self.n2))):
-                        self.take(self.place(oc, o, o2))
+                arrived(self.buf.at[pl.ds(oc * pieces, pieces)], self.recv.at[2 * self.n1])
 
         def run(*pairs):
             live = list(pairs)
@@ -192,7 +190,7 @@
         load_f.wait()
         f_copy.wait_recv()
         wag[slot(c, x, y)] = jnp.concatenate([fpc[0], fpc[1]], axis=1).astype(BF16)
-        weights_gather = Gather(wag, wsend, wrecv, ny, across_y, nx, across_x, slot_y)
+        weights_gather = Gather(wag, wsend, wrecv, ny, at_y, across_y, nx, across_x, slot_y)
         weights_gather.start1()
         weights_gather.start2()
         load_v.wait()
@@ -203,16 +201,19 @@
         run((weights_gather.relay2(), 1))
 
         def forward(b, kind, buf):
-            for o in far_first(nz) + [0]:
-                zs = lax.rem(z - o + nz, nz)
-                mine = buf.at[b, c, zs]
-                z_wait(kind, b, mine, zs)
-                remote(mine, mine, fsend.at[b, kind], frecv.at[b, kind, zs], {"c": oc}).start()
+            if (kind, b) == (1, 0):
+                for o in far_first(nz) + [0]:
+                    zs = lax.rem(z - o + nz, nz)
+                    mine = buf.at[b, c, zs]
+                    arrived(mine, zfirst.at[zs])
+                    remote(mine, mine, fsend.at[b, kind], frecv.at[b, kind], {"c": oc}).start()
+            else:
+                mine = buf.at[b, c]
+                arrived(mine, zall.at[kind, b])
+                remote(mine, mine, fsend.at[b, kind], frecv.at[b, kind], {"c": oc}).start()
 
         def forwarded(b, kind, buf):
-            for zs in range(nz):
-                other = buf.at[b, oc, zs]
-                remote(other, other, fsend.at[b, kind], frecv.at[b, kind, zs], {"c": oc}).wait_recv()
+            arrived(buf.at[b, oc], frecv.at[b, kind])
 
         count = nz * tokens
 
@@ -271,7 +272,7 @@
                         t = self.at1(o1)
                         remote(
                             self.send.at[t, end], self.land.at[o1 - 1, end],
-                            self.sem1, self.recv1.at[o1 - 1, end], {self.name1: t},
+                            self.sem1, self.recv1.at[end], {self.name1: t},
                         ).start()
 
             def steps(self, result, where):
@@ -279,22 +280,19 @@
                 for o in far_first(self.n2) + [0]:
                     end = self.at2(o)
                     total = self.send[self.me1, end].astype(F32)
+                    arrived(self.land.at[:, end], self.recv1.at[end])
                     for o1 in range(1, self.n1):
-                        land = self.land.at[o1 - 1, end]
-                        remote(land, land, self.sem1, self.recv1.at[o1 - 1, end], {"c": oc}).wait_recv()
-                        total = total + land[...].astype(F32)
+                        total = total + self.land[o1 - 1, end].astype(F32)
                     if o:
                         self.send2[o - 1] = total.astype(BF16)
                         remote(
                             self.send2.at[o - 1], self.land2.at[o - 1],
-                            self.sem2, self.recv2.at[o - 1], {self.name2: end},
+                            self.sem2, self.recv2, {self.name2: end},
                         ).start()
                     yield
+                arrived(self.land2, self.recv2)
                 for o in far_first(self.n2):
-                    land = self.land2.at[o - 1]
-                    remote(land, land, self.sem2, self.recv2.at[o - 1], {"c": oc}).wait_recv()
-                    total = total + land[...].astype(F32)
-                    yield
+                    total = total + self.land2[o - 1].astype(F32)
                 result[where] = total.astype(BF16)
 
         def sums(b):
@@ -317,8 +315,8 @@
             first, second = sums(b)
             own = slot(c, x, y)
             run((first.steps(a_all.at[b], own), 2), (second.steps(b_all.at[b], own), 1))
-            ga = Gather(a_all.at[b], a_sem3.at[b], a_recv3.at[b], ny, across_y, nx, across_x, slot_y)
-            gb = Gather(b_all.at[b], b_sem3.at[b], b_recv3.at[b], nx, across_x, ny, across_y, slot_x)
+            ga = Gather(a_all.at[b], a_sem3.at[b], a_recv3.at[b], ny, at_y, across_y, nx, across_x, slot_y)
+            gb = Gather(b_all.at[b], b_sem3.at[b], b_recv3.at[b], nx, at_x, across_x, ny, across_y, slot_x)
             ga.start1()
             gb.start1()
             ga.start2()
@@ -387,8 +385,7 @@
                 for each in range(blocks):
                     send_queries(each)
             else:
-                for zs in range(nz):
-                    z_wait(2, b - 1, qbuf.at[b - 1, zs], zs)
+                arrived(qbuf.at[b - 1], zall.at[2, b - 1])
                 answer(b - 1)
             finish_reduce(b)
             if b + 1 < blocks:
@@ -400,8 +397,7 @@
                 forwarded(b + 1, 0, kbuf)
                 keys_part(b + 1, oc)
         last = blocks - 1
-        for zs in range(nz):
-            z_wait(2, last, qbuf.at[last, zs], zs)
+        arrived(qbuf.at[last], zall.at[2, last])
         answer(last)
 
         def sent(ref, sem):
@@ -446,25 +442,26 @@
         pltpu.VMEM((2, nz * tokens, 3 * half), BF16),
         pltpu.VMEM((2, nz * tokens, half), F32),
         pltpu.VMEM((2, nz * tokens, half), F32),
-        dma((3, blocks, nz)),
         dma((3, blocks)),
-        dma((blocks, 2, nz)),
+        dma((nz,)),
+        dma((3, blocks)),
+        dma((blocks, 2)),
         dma((blocks, 2)),
         dma((3,)),
         dma((2,)),
-        dma((2 * pieces,)),
+        dma((2 * ny + 1,)),
         dma(()),
-        dma((blocks, nx - 1, ny)),
-        dma((blocks,)),
-        dma((blocks, ny - 1)),
-        dma((blocks,)),
-        dma((blocks, 2 * pieces)),
-        dma((blocks,)),
-        dma((blocks, ny - 1, nx)),
-        dma((blocks,)),
-        dma((blocks, nx - 1)),
-        dma((blocks,)),
-        dma((blocks, 2 * pieces)),
+        dma((blocks, ny)),
+        dma((blocks,)),
+        dma((blocks,)),
+        dma((blocks,)),
+        dma((blocks, 2 * ny + 1)),
+        dma((blocks,)),
+        dma((blocks, nx)),
+        dma((blocks,)),
+        dma((blocks,)),
+        dma((blocks,)),
+        dma((blocks, 2 * nx + 1)),
         dma((blocks,)),
     ]
     return kernel, scratch

time: 78.9 us -> 74.8 us (0.948)
  Pallas kernels: 77.9 us -> 73.9 us
    pallas_call x1, Pallas kernels: 77.9 us -> 73.9 us  [local(): pl.pallas_call(kernel, out_shape=pltpu.VMEM((blocks, nz * tokens, hd), BF...]
where the time goes in v3:
time: 74.8 us; the launch traced here: 74.7 us
  Pallas kernels  73.9 us (99%)
  local copies, waits for them, and re-layouts  0.8 us (1%)
    pallas_call x1, Pallas kernels, local(): pl.pallas_call(kernel, out_shape=pltpu.VMEM((blocks, nz * tokens, hd), BF...  73.9 us

profile of v3, /device:TPU:1, one launch (start us, length us, event | category | flops | bytes accessed | tf_op | source)
XLA Modules:
  0.0 74.7 jit_solution(10075637537151485040)
XLA Ops:
  0.0 73.9 %shard_map.55 = bf16[2,256,512]{2,1,0:T(8,128)(2,1)S(1)} custom-call(bf16[2,32,4096]{2,1,0:T(8,128)(2,1)} %q_hbm.1, bf16[2,32,4096]{2,1,0:T(8,128)(2,1)} %k_hbm.1, bf16[2,32,4096]{2,1,0:T(8,128)(2,1)} %v_hbm.1, bf16[2,8,32]{2,1,0:T(8,128)(2,1)} %bitcast.1, f32[1,3,8,256]{3,2,1,0:T(8,128)} %f_hbm.1), custom_call_target="tpu_custom_call" | custom-call | tf_op jit(solution)/shard_map/pallas_call | solution.py:478
  73.9 0.8 %copy.7 = bf16[2,256,512]{2,1,0:T(8,128)(2,1)} copy(bf16[2,256,512]{2,1,0:T(8,128)(2,1)S(1)} %shard_map.55) | data formatting | bytes 1048576

commit v4 on v3

--- a/solution.py
+++ b/solution.py
@@ -323,7 +323,8 @@
             gb.start2()
             run((gb.relay1(), 1))
             run((ga.relay1(), 1))
-            run((ga.relay2(), 1), (gb.relay2(), 1))
+            run((gb.relay2(), 1))
+            run((ga.relay2(), 1))
             ga.end()
             gb.end()
 

time: 74.8 us -> 74.8 us (level)
  no operation moved by 1% of the time
where the time goes in v4:
time: 74.8 us; the launch traced here: 74.7 us
  Pallas kernels  73.9 us (99%)
  local copies, waits for them, and re-layouts  0.8 us (1%)
    pallas_call x1, Pallas kernels, local(): pl.pallas_call(kernel, out_shape=pltpu.VMEM((blocks, nz * tokens, hd), BF...  73.9 us

profile of v4, /device:TPU:1, one launch (start us, length us, event | category | flops | bytes accessed | tf_op | source)
XLA Modules:
  0.0 74.7 jit_solution(18119840038358604404)
XLA Ops:
  0.0 73.9 %shard_map.55 = bf16[2,256,512]{2,1,0:T(8,128)(2,1)S(1)} custom-call(bf16[2,32,4096]{2,1,0:T(8,128)(2,1)} %q_hbm.1, bf16[2,32,4096]{2,1,0:T(8,128)(2,1)} %k_hbm.1, bf16[2,32,4096]{2,1,0:T(8,128)(2,1)} %v_hbm.1, bf16[2,8,32]{2,1,0:T(8,128)(2,1)} %bitcast.1, f32[1,3,8,256]{3,2,1,0:T(8,128)} %f_hbm.1), custom_call_target="tpu_custom_call" | custom-call | tf_op jit(solution)/shard_map/pallas_call | solution.py:479
  73.9 0.8 %copy.7 = bf16[2,256,512]{2,1,0:T(8,128)(2,1)} copy(bf16[2,256,512]{2,1,0:T(8,128)(2,1)S(1)} %shard_map.55) | data formatting | bytes 1048576
